TPU v7x, 32 devices: a whole 2x2x4 slice. The times are simulated.
32 devices in a mesh: layer: 2 (over core), row: 4 (over z), rep: 4 (over y, x).
Axes of the slice: x: 2, y: 2, z: 4, core: 2. Of those that a mesh axis runs over, the one named last changes fastest.
Arguments:
- features: bfloat16 [2048, 256], P(('row', 'rep')), may hold values from -6 to 6
- class_ids: int32 [2048], P(('row', 'rep')), may hold values from 0 to 256
- label_table: bfloat16 [256, 256], replicated, may hold values from -3 to 3
- self_weight: bfloat16 [2, 256, 256], P('layer'), may hold values from -0.375 to 0.375
- neighbor_weight: bfloat16 [2, 256, 256], P('layer'), may hold values from -0.375 to 0.375
- norm_scale: float32 [256], replicated, may hold values from 0.1 to 1.9
- tile_values: bfloat16 [4, 4, 32, 128, 128], P('row', 'rep')
- tile_block_row: int32 [4, 4, 32], P('row', 'rep'), may hold values from 0 to 3, as said below
- tile_section: int32 [4, 4, 32], P('row', 'rep'), may hold values from 0 to 3
- tile_count: int32 [4, 4], P('row', 'rep'), may hold values from 4 to 32, as said below
Outputs:
- hidden_states: bfloat16 [2, 2048, 256], P('layer', ('row', 'rep'))
Inputs may be any that keep to these rules, and one draw needn't show every extreme that they name: `class_ids`: 256 marks a node without a label. `tile_block_row`: slots 0 to 3 of every device name block rows 0 to 3 in order. `tile_count`: at least 4; 32 on some device.
All inputs are finite; a program needn't handle non-finite values.
Results may differ from a plain program's by a relative error of at most 0.0052.
Values may be sent and summed in bfloat16 or wider, within the bound.
No kernel may reach another device: no remote copies, remote signals or barrier semaphores. Data moves between devices by JAX's collectives and lax.ppermute only.
A program may use at most 64 MiB of HBM per device.

v0:
```python
import jax
import jax.numpy as jnp
from jax import lax
from jax.sharding import PartitionSpec as P


def shifted(value, axis, steps):
    count = lax.axis_size(axis)
    leading, last = (max(0, -steps), min(count, count - steps))
    return lax.ppermute(value, axis, [(source, source + steps) for source in range(leading, last)])


def settle(mixture, norm_scale, first):
    if first:
        active = jnp.maximum(mixture, 0.0)
        center = active - jnp.mean(active, axis=-1, keepdims=True)
        spread = jnp.mean(center * center, axis=-1, keepdims=True)
        return (center * lax.rsqrt(spread + 1e-05) * norm_scale).astype(jnp.bfloat16)
    return mixture.astype(jnp.bfloat16)


def body(
    features,
    class_ids,
    label_table,
    self_weight,
    neighbor_weight,
    norm_scale,
    tile_values,
    tile_block_row,
    tile_section,
    tile_count,
):
    which_layer = lax.axis_index("layer")
    groups = lax.axis_size("row")
    splits = lax.axis_size("rep")
    tile_data = tile_values[0, 0]
    block_rows = tile_block_row[0, 0]
    sections = tile_section[0, 0]
    filled = tile_count[0, 0]
    slot_total = tile_data.shape[0]
    tile_edge = tile_data.shape[1]
    hidden_dim = features.shape[1]
    classes = label_table.shape[0]
    one_hot = (class_ids[:, None] == jnp.arange(classes, dtype=jnp.int32)[None, :]).astype(
        jnp.bfloat16
    )
    inputs = (
        features.astype(jnp.float32)
        + jnp.dot(one_hot, label_table, preferred_element_type=jnp.float32)
    ).astype(jnp.bfloat16)
    slot_ids = jnp.arange(slot_total, dtype=jnp.int32)
    targets = jnp.arange(splits, dtype=jnp.int32)

    def placement(keep_mask):
        live = jnp.logical_and(slot_ids < filled, keep_mask)
        return jnp.logical_and(block_rows[None, :] == targets[:, None], live[None, :]).astype(
            jnp.float32
        )

    outcomes = []
    all_slots = slot_ids >= 0
    tile_sums = jnp.sum(tile_data, axis=-1, dtype=jnp.float32)
    row_sums = jnp.dot(placement(all_slots), tile_sums, precision=lax.Precision.HIGHEST).reshape(
        splits * tile_edge
    )
    current = inputs
    for layer_no in range(2):
        gathered = lax.all_gather(current, "row", axis=0, tiled=True)
        panel_rows = gathered.reshape(groups, tile_edge, hidden_dim)
        weights_on = placement(all_slots)

        def add_tiles(batch_no, running):
            offset = batch_no * 8
            tile_batch = lax.dynamic_slice_in_dim(tile_data, offset, 8, 0)
            where_from = lax.dynamic_slice_in_dim(sections, offset, 8, 0)
            onto_rows = lax.dynamic_slice_in_dim(weights_on, offset, 8, 1)
            sources = panel_rows[where_from]
            products = jnp.einsum(
                "kab,kbf->kaf", tile_batch, sources, preferred_element_type=jnp.float32
            )
            return running + jnp.einsum(
                "sk,kaf->saf", onto_rows, products, precision=lax.Precision.HIGHEST
            )

        running = jnp.zeros((splits, tile_edge, hidden_dim), jnp.float32)
        running = lax.fori_loop(0, slot_total // 8, add_tiles, running)
        partial_value = running.reshape(splits * tile_edge, hidden_dim)
        if layer_no == 0:
            summed, degree = (
                lax.psum_scatter(partial_value, "rep", scatter_dimension=0, tiled=True),
                lax.psum_scatter(row_sums, "rep", scatter_dimension=0, tiled=True),
            )
        else:
            summed = lax.psum_scatter(partial_value, "rep", scatter_dimension=0, tiled=True)
        neighbor = (summed * lax.rsqrt(degree)[:, None]).astype(jnp.bfloat16)
        mixture = jnp.dot(current, self_weight[0], preferred_element_type=jnp.float32) + jnp.dot(
            neighbor, neighbor_weight[0], preferred_element_type=jnp.float32
        )
        result = jnp.where(
            which_layer == 0, settle(mixture, norm_scale, True), settle(mixture, norm_scale, False)
        )
        outcomes.append(result)
        if layer_no == 0:
            current = shifted(result, "layer", 1)
    selected = jnp.where(which_layer == 0, outcomes[0], outcomes[1])
    return selected[None]


def solution(mesh):
    return jax.shard_map(
        body,
        mesh=mesh,
        in_specs=(
            P(("row", "rep"), None),
            P(("row", "rep")),
            P(),
            P("layer", None, None),
            P("layer", None, None),
            P(),
            P("row", "rep", None, None, None),
            P("row", "rep", None),
            P("row", "rep", None),
            P("row", "rep"),
        ),
        out_specs=P("layer", ("row", "rep"), None),
        check_vma=False,
    )
```

profile of v0, /device:TPU:0, one launch (start us, length us, event | category | flops | bytes accessed | tf_op | source)
XLA Modules:
  0.0 137.9 jit_solution(1256336047873248968)
XLA Ops:
  7.2 1.1 fusion.14
  8.4 15.7 %all_gather.6 = bf16[512,256]{1,0:T(8,128)(2,1)S(1)} all-gather(bf16[128,256]{1,0:T(8,128)(2,1)S(1)} %fusion.14), channel_id=1, replica_groups=mesh['layer'=2,'row'=4,'rep'=4] {'row'}, dimensions={0}, use_global_device_ids=true | all-gather | bytes 327680 | tf_op jit(solution)/shard_map/all_gather | solution.py:69
  24.7 17.7 %while.28 = (s32[]{:T(128)}, f32[4,128,256]{2,0,1:T(4,128)S(1)}, f32[4,32]{1,0:T(4,128)S(1)}, bf16[32,128,128]{2,1,0:T(8,128)(2,1)}, s32[32]{0:T(128)}, /*index=...) while((s32[]{:T(128)}, f32[4,128,256]{2,0,1:T(4,128)S(1)}, ...), condition=%wide.region_1.0_spmd.clone, body=%wide.region_0.0_spmd.clone.sunk | while | flops 79954976 | bytes 4985641 | solution.py:87
  26.0 1.2 fusion.53
  27.3 1.8 %convolution_add_fusion.7 = f32[4,128,256]{2,0,1:T(4,128)S(1)} fusion(f32[8,128,256]{2,1,0:T(8,128)S(1)} %fusion.53, f32[4,128,256]{2,0,1:T(4,128)S(1)} %get-tuple-element.380, pred[]{:T(512)S(6)} %compare.6, f32[4,32]{1,0:T(4,128)S(1)} %get-tuple-element.391, s32[]{:T(128)S(6)} %select_n.78), kind=kOutput, calls=%fused_computation.2.clone.1 | convolution fusion | flops 12845056 | bytes 2097669 | tf_op jit(solution)/shard_map/while/body/eval_jaxpr/sk,kaf->saf/dot_general | solution.py:82
  29.1 0.7 compare_select_fusion.4
  30.5 1.2 fusion.53
  31.7 1.8 %convolution_add_fusion.7 = f32[4,128,256]{2,0,1:T(4,128)S(1)} fusion(f32[8,128,256]{2,1,0:T(8,128)S(1)} %fusion.53, f32[4,128,256]{2,0,1:T(4,128)S(1)} %get-tuple-element.380, pred[]{:T(512)S(6)} %compare.6, f32[4,32]{1,0:T(4,128)S(1)} %get-tuple-element.391, s32[]{:T(128)S(6)} %select_n.78), kind=kOutput, calls=%fused_computation.2.clone.1 | convolution fusion | flops 12845056 | bytes 2097669 | tf_op jit(solution)/shard_map/while/body/eval_jaxpr/sk,kaf->saf/dot_general | solution.py:82
  33.6 0.7 compare_select_fusion.4
  34.9 1.2 fusion.53
  36.2 1.8 %convolution_add_fusion.7 = f32[4,128,256]{2,0,1:T(4,128)S(1)} fusion(f32[8,128,256]{2,1,0:T(8,128)S(1)} %fusion.53, f32[4,128,256]{2,0,1:T(4,128)S(1)} %get-tuple-element.380, pred[]{:T(512)S(6)} %compare.6, f32[4,32]{1,0:T(4,128)S(1)} %get-tuple-element.391, s32[]{:T(128)S(6)} %select_n.78), kind=kOutput, calls=%fused_computation.2.clone.1 | convolution fusion | flops 12845056 | bytes 2097669 | tf_op jit(solution)/shard_map/while/body/eval_jaxpr/sk,kaf->saf/dot_general | solution.py:82
  38.0 0.7 compare_select_fusion.4
  39.3 1.2 fusion.53
  40.6 1.8 %convolution_add_fusion.7 = f32[4,128,256]{2,0,1:T(4,128)S(1)} fusion(f32[8,128,256]{2,1,0:T(8,128)S(1)} %fusion.53, f32[4,128,256]{2,0,1:T(4,128)S(1)} %get-tuple-element.380, pred[]{:T(512)S(6)} %compare.6, f32[4,32]{1,0:T(4,128)S(1)} %get-tuple-element.391, s32[]{:T(128)S(6)} %select_n.78), kind=kOutput, calls=%fused_computation.2.clone.1 | convolution fusion | flops 12845056 | bytes 2097669 | tf_op jit(solution)/shard_map/while/body/eval_jaxpr/sk,kaf->saf/dot_general | solution.py:82
  42.5 0.9 copy.15
  45.1 9.9 %all-reduce = f32[512]{0:T(512)S(1)} all-reduce(f32[512]{0:T(512)S(1)} %convolution_bitcast_fusion), channel_id=3, replica_groups=mesh['layer'=2,'row'=4,'rep'=4] {'rep'}, use_global_device_ids=true, to_apply=%region_4.0.clone | all-reduce | flops 512 | bytes 4096
  55.3 14.9 %reduce-scatter.3.cloned.1.call-done = f32[128,256]{1,0:T(8,128)} async-done(((f32[512,256]{1,0:T(8,128)}), f32[128,256]{1,0:T(8,128)}) %reduce-scatter.3.cloned.1.call-update) | async-done | bytes 131088 | tf_op jit(solution)/shard_map/reduce_scatter | solution.py:91
  70.2 1.2 maximum_reduce_fusion.1
  71.7 1.4 collective-permute-start
  73.1 0.9 collective-permute-done
  74.0 14.0 %all_gather.7 = bf16[512,256]{1,0:T(8,128)(2,1)S(1)} all-gather(bf16[128,256]{1,0:T(8,128)(2,1)S(1)} %collective-permute-done), channel_id=1, replica_groups=mesh['layer'=2,'row'=4,'rep'=4] {'row'}, dimensions={0}, use_global_device_ids=true | all-gather | bytes 327680 | tf_op jit(solution)/shard_map/all_gather | solution.py:69
  88.0 13.9 %while.29 = (s32[]{:T(128)}, f32[4,128,256]{2,0,1:T(4,128)S(1)}, f32[4,32]{1,0:T(4,128)S(1)}, bf16[32,128,128]{2,1,0:T(8,128)(2,1)S(1)}, s32[32]{0:T(128)}, /*in...) while((s32[]{:T(128)}, f32[4,128,256]{2,0,1:T(4,128)S(1)}, ...), condition=%wide.region_8.9_spmd.clone, body=%wide.region_7.8_spmd.clone.sunk | while | flops 79954976 | bytes 4985641 | solution.py:87
  89.6 1.8 %convolution_add_fusion.8 = f32[4,128,256]{2,0,1:T(4,128)S(1)} fusion(f32[8,128,256]{2,1,0:T(8,128)S(1)} %fusion.58, f32[4,128,256]{2,0,1:T(4,128)S(1)} %get-tuple-element.410, pred[]{:T(512)S(6)} %compare.7, f32[4,32]{1,0:T(4,128)S(1)} %get-tuple-element.421, s32[]{:T(128)S(6)} %select_n.80), kind=kOutput, calls=%fused_computation.12.clone.1 | convolution fusion | flops 12845056 | bytes 2097669 | tf_op jit(solution)/shard_map/while/body/eval_jaxpr/sk,kaf->saf/dot_general | solution.py:82
  91.5 0.7 compare_select_fusion.5
  93.1 1.8 %convolution_add_fusion.8 = f32[4,128,256]{2,0,1:T(4,128)S(1)} fusion(f32[8,128,256]{2,1,0:T(8,128)S(1)} %fusion.58, f32[4,128,256]{2,0,1:T(4,128)S(1)} %get-tuple-element.410, pred[]{:T(512)S(6)} %compare.7, f32[4,32]{1,0:T(4,128)S(1)} %get-tuple-element.421, s32[]{:T(128)S(6)} %select_n.80), kind=kOutput, calls=%fused_computation.12.clone.1 | convolution fusion | flops 12845056 | bytes 2097669 | tf_op jit(solution)/shard_map/while/body/eval_jaxpr/sk,kaf->saf/dot_general | solution.py:82
  96.6 1.8 %convolution_add_fusion.8 = f32[4,128,256]{2,0,1:T(4,128)S(1)} fusion(f32[8,128,256]{2,1,0:T(8,128)S(1)} %fusion.58, f32[4,128,256]{2,0,1:T(4,128)S(1)} %get-tuple-element.410, pred[]{:T(512)S(6)} %compare.7, f32[4,32]{1,0:T(4,128)S(1)} %get-tuple-element.421, s32[]{:T(128)S(6)} %select_n.80), kind=kOutput, calls=%fused_computation.12.clone.1 | convolution fusion | flops 12845056 | bytes 2097669 | tf_op jit(solution)/shard_map/while/body/eval_jaxpr/sk,kaf->saf/dot_general | solution.py:82
  98.4 0.7 compare_select_fusion.5
  100.1 1.8 %convolution_add_fusion.8 = f32[4,128,256]{2,0,1:T(4,128)S(1)} fusion(f32[8,128,256]{2,1,0:T(8,128)S(1)} %fusion.58, f32[4,128,256]{2,0,1:T(4,128)S(1)} %get-tuple-element.410, pred[]{:T(512)S(6)} %compare.7, f32[4,32]{1,0:T(4,128)S(1)} %get-tuple-element.421, s32[]{:T(128)S(6)} %select_n.80), kind=kOutput, calls=%fused_computation.12.clone.1 | convolution fusion | flops 12845056 | bytes 2097669 | tf_op jit(solution)/shard_map/while/body/eval_jaxpr/sk,kaf->saf/dot_general | solution.py:82
  101.9 0.9 copy.16
  102.9 25.8 %reduce-scatter.5.cloned.1.call-done = f32[128,256]{1,0:T(8,128)} async-done(((f32[512,256]{1,0:T(8,128)}), f32[128,256]{1,0:T(8,128)}) %reduce-scatter.5.cloned.1.call-update) | async-done | bytes 131088 | tf_op jit(solution)/shard_map/reduce_scatter | solution.py:95
  128.7 1.1 fusion.15
  130.3 0.8 fusion.24
  (74 shorter events, 10.9 us)
Async XLA Ops:
  6.5 63.6 %copy-start = (bf16[1,256,256]{2,1,0:T(8,128)(2,1)S(1)}, bf16[1,256,256]{2,1,0:T(8,128)(2,1)}, u32[]{:S(2)}) copy-start(bf16[1,256,256]{2,1,0:T(8,128)(2,1)} %param.18) | copy-start | bytes 393220
  6.5 63.6 %reduce-scatter.3.cloned.1.call-start = ((), (), s32[]{:S(2)}) async-start(), calls=%async_computation.2 | async-start | bytes 655360 | tf_op jit(solution)/shard_map/reduce_scatter | solution.py:91
  8.4 16.3 %copy-start.4 = (bf16[128,256]{1,0:T(8,128)(2,1)}, bf16[128,256]{1,0:T(8,128)(2,1)S(1)}, u32[]{:S(2)}) copy-start(bf16[128,256]{1,0:T(8,128)(2,1)S(1)} %fusion.14) | copy-start | bytes 196612
  42.4 1.0 copy-start.14
  42.5 2.2 %copy-start.1 = (bf16[32,128,128]{2,1,0:T(8,128)(2,1)S(1)}, bf16[32,128,128]{2,1,0:T(8,128)(2,1)}, u32[]{:S(2)}) copy-start(bf16[32,128,128]{2,1,0:T(8,128)(2,1)} %get-tuple-element.431) | copy-start | bytes 3145732
  43.4 1.6 %copy-start.11 = (s32[1,1,32]{2,1,0:T(1,128)S(1)}, s32[1,1,32]{2,1,0:T(1,128)}, u32[]{:S(2)}) copy-start(s32[1,1,32]{2,1,0:T(1,128)} %param.21) | copy-start | bytes 388
  43.4 11.8 %copy-start.5 = (bf16[128,256]{1,0:T(8,128)(2,1)S(1)}, bf16[128,256]{1,0:T(8,128)(2,1)}, u32[]{:S(2)}) copy-start(bf16[128,256]{1,0:T(8,128)(2,1)} %copy-done.4) | copy-start | bytes 196612
  43.4 11.8 %copy-start.6 = (bf16[1,256,256]{2,1,0:T(8,128)(2,1)S(1)}, bf16[1,256,256]{2,1,0:T(8,128)(2,1)}, u32[]{:S(2)}) copy-start(bf16[1,256,256]{2,1,0:T(8,128)(2,1)} %param.17) | copy-start | bytes 393220
  43.4 85.3 %reduce-scatter.5.cloned.1.call-start = ((), (), s32[]{:S(2)}) async-start(), calls=%async_computation.3 | async-start | bytes 655360 | tf_op jit(solution)/shard_map/reduce_scatter | solution.py:95
  43.4 28.2 %copy-start.10 = (f32[256]{0:T(256)S(1)}, f32[256]{0:T(256)}, u32[]{:S(2)}) copy-start(f32[256]{0:T(256)} %param.19) | copy-start | bytes 3076
  55.2 16.6 %copy-start.12 = (f32[128]{0:T(128)}, f32[128]{0:T(128)S(1)}, u32[]{:S(2)}) copy-start(f32[128]{0:T(128)S(1)} %dynamic-slice_rsqrt_fusion) | copy-start | bytes 1540
  71.4 16.6 %copy-start.2 = (f32[128,256]{1,0:T(8,128)}, f32[128,256]{1,0:T(8,128)S(1)}, u32[]{:S(2)}) copy-start(f32[128,256]{1,0:T(8,128)S(1)} %get-tuple-element.292) | copy-start | bytes 393220
  71.7 2.2 %collective-permute-start = (bf16[128,256]{1,0:T(8,128)(2,1)S(1)}, bf16[128,256]{1,0:T(8,128)(2,1)S(1)}, u32[]{:S(2)}, u32[]{:S(2)}) collective-permute-start(bf16[128,256]{1,0:T(8,128)(2,1)S(1)} %fusion.21), channel_id=1, source_target_pairs={{0,16},{1,17},{2,18},{3,19},{4,20},{5,21},{6,22},{7,23},{8,24},{9,... | collective-permute-start | bytes 196616 | tf_op jit(solution)/shard_map/ppermute | solution.py:10
  74.0 14.0 %copy-start.8 = (bf16[128,256]{1,0:T(8,128)(2,1)}, bf16[128,256]{1,0:T(8,128)(2,1)S(1)}, u32[]{:S(2)}) copy-start(bf16[128,256]{1,0:T(8,128)(2,1)S(1)} %collective-permute-done) | copy-start | bytes 196612
  101.9 26.8 %copy-start.13 = (f32[128]{0:T(128)S(1)}, f32[128]{0:T(128)}, u32[]{:S(2)}) copy-start(f32[128]{0:T(128)} %copy-done.12) | copy-start | bytes 1540
  101.9 27.9 %copy-start.7 = (bf16[1,256,256]{2,1,0:T(8,128)(2,1)S(1)}, bf16[1,256,256]{2,1,0:T(8,128)(2,1)}, u32[]{:S(2)}) copy-start(bf16[1,256,256]{2,1,0:T(8,128)(2,1)} %param.17) | copy-start | bytes 393220
  101.9 27.9 %copy-start.9 = (bf16[128,256]{1,0:T(8,128)(2,1)S(1)}, bf16[128,256]{1,0:T(8,128)(2,1)}, u32[]{:S(2)}) copy-start(bf16[128,256]{1,0:T(8,128)(2,1)} %copy-done.8) | copy-start | bytes 196612
  101.9 28.3 %copy-start.3 = (f32[128,256]{1,0:T(8,128)S(1)}, f32[128,256]{1,0:T(8,128)}, u32[]{:S(2)}) copy-start(f32[128,256]{1,0:T(8,128)} %copy-done.2) | copy-start | bytes 393220
Sparse Core Ops, SparseCore 0:
  43.5 26.6 reduce-scatter.2
  103.0 25.6 reduce-scatter.4
where the time goes:
time: 138 us
  waiting for transfers between devices  41.6 us (30%)
  blocking collectives  39.6 us (29%)
  matrix products  24.8 us (18%)
  between operations  14.9 us (11%)
  other arithmetic  8.2 us (6%)
  local copies, waits for them, and re-layouts  7.15 us (5%)
  starting transfers between devices  1.4 us (1%)
    reduce_scatter x2, waiting for transfers between devices, body(): lax.psum_scatter(partial_value, 'rep', scatter_dimension=0, tiled=True)  40.7 us
    all_gather x2, blocking collectives, body(): gathered = lax.all_gather(current, 'row', axis=0, tiled=True)  29.7 us
    dot_general x8, matrix products, add_tiles(): jnp.einsum('sk,kaf->saf', onto_rows, products, precision=lax.Precision.HI...  14.8 us
    unnamed x1, blocking collectives  9.94 us
    dot_general x8, matrix products, add_tiles(): jnp.einsum('kab,kbf->kaf', tile_batch, sources, preferred_element_type=jn...  6.1 us
    select_n x8, other arithmetic, add_tiles(): sources = panel_rows[where_from]  5.87 us
    gather x8, local copies, waits for them, and re-layouts, add_tiles(): sources = panel_rows[where_from]  4.63 us
  transfers between devices with their start and end apart: 3, of which 3 were waited for; matrix products, arithmetic and copies ran while one was open for 1% of the time, Pallas kernels for 0%

commit v1 on v0

--- a/solution.py
+++ b/solution.py
@@ -66,7 +66,14 @@
     )
     current = inputs
     for layer_no in range(2):
-        gathered = lax.all_gather(current, "row", axis=0, tiled=True)
+        n_dev = lax.axis_size("row")
+        right = [(i, (i + 1) % n_dev) for i in range(n_dev)]
+        pieces = [current]
+        for far in range(1, n_dev):
+            pieces = [lax.ppermute(pieces[0], "row", right), *pieces]
+        whole = jnp.concatenate(pieces, axis=0)
+        shift = (lax.axis_index("row") + 1) * pieces[-1].shape[0]
+        gathered = jnp.roll(whole, shift, axis=0)
         panel_rows = gathered.reshape(groups, tile_edge, hidden_dim)
         weights_on = placement(all_slots)
 

time: 138 us -> 143 us (1.036)
  blocking collectives: 39.6 us -> 10.2 us
  waiting for transfers between devices: 41.6 us -> 66.9 us
  other arithmetic: 8.2 us -> 12.9 us
  starting transfers between devices: 1.4 us -> 6.03 us
    ppermute x0 -> x6, waiting for transfers between devices: none -> 31.8 us  [body(): pieces = [lax.ppermute(pieces[0], 'row', right), *pieces]]
    all_gather x2 -> x0, blocking collectives: 29.7 us -> none  [body(): gathered = lax.all_gather(current, 'row', axis=0, tiled=True)]
    reduce_scatter x2, waiting for transfers between devices: 40.7 us -> 34.1 us  [body(): lax.psum_scatter(partial_value, 'rep', scatter_dimension=0, tiled=True)]
    concatenate x0 -> x2, other arithmetic: none -> 4.64 us  [body(): gathered = jnp.roll(whole, shift, axis=0)]
    ppermute x0 -> x6, starting transfers between devices: none -> 4.62 us  [body(): pieces = [lax.ppermute(pieces[0], 'row', right), *pieces]]
  transfers between devices with their start and end apart: 3 -> 9, of which waited for: 3 -> 9; matrix products, arithmetic and copies ran while one was open for 1% -> 1% of each run, Pallas kernels for 0% -> 0%
where the time goes in v1:
time: 143 us
  waiting for transfers between devices  66.9 us (47%)
  matrix products  24.8 us (17%)
  between operations  14.9 us (10%)
  other arithmetic  12.9 us (9%)
  blocking collectives  10.2 us (7%)
  local copies, waits for them, and re-layouts  7.13 us (5%)
  starting transfers between devices  6.03 us (4%)
    reduce_scatter x2, waiting for transfers between devices, body(): lax.psum_scatter(partial_value, 'rep', scatter_dimension=0, tiled=True)  34.1 us
    ppermute x6, waiting for transfers between devices, body(): pieces = [lax.ppermute(pieces[0], 'row', right), *pieces]  31.8 us
    dot_general x8, matrix products, add_tiles(): jnp.einsum('sk,kaf->saf', onto_rows, products, precision=lax.Precision.HI...  14.7 us
    unnamed x1, blocking collectives  10.2 us
    dot_general x8, matrix products, add_tiles(): jnp.einsum('kab,kbf->kaf', tile_batch, sources, preferred_element_type=jn...  6.09 us
    select_n x8, other arithmetic, add_tiles(): sources = panel_rows[where_from]  5.87 us
    concatenate x2, other arithmetic, body(): gathered = jnp.roll(whole, shift, axis=0)  4.64 us
    gather x8, local copies, waits for them, and re-layouts, add_tiles(): sources = panel_rows[where_from]  4.63 us
  transfers between devices with their start and end apart: 9, of which 9 were waited for; matrix products, arithmetic and copies ran while one was open for 1% of the time, Pallas kernels for 0%

profile of v1, /device:TPU:0, one launch (start us, length us, event | category | flops | bytes accessed | tf_op | source)
XLA Modules:
  0.0 143.0 jit_solution(16432419306355666509)
XLA Ops:
  6.5 1.2 fusion.14
  7.7 3.1 %collective-permute-start = (bf16[128,256]{1,0:T(8,128)(2,1)S(1)}, bf16[128,256]{1,0:T(8,128)(2,1)S(1)}, u32[]{:S(2)}, u32[]{:S(2)}) collective-permute-start(bf16[128,256]{1,0:T(8,128)(2,1)S(1)} %fusion.14), channel_id=1, source_target_pairs={{0,4},{4,8},{8,12},{12,0},{1,5},{5,9},{9,13},{13,1},{2,6},{6,10},{... | collective-permute-start | bytes 196616 | tf_op jit(solution)/shard_map/ppermute | solution.py:73
  11.5 3.6 %collective-permute-done = bf16[128,256]{1,0:T(8,128)(2,1)S(1)} collective-permute-done((bf16[128,256]{1,0:T(8,128)(2,1)S(1)}, bf16[128,256]{1,0:T(8,128)(2,1)S(1)}, u32[]{:S(2)}, u32[]{:S(2)}) %collective-permute-start) | collective-permute-done | bytes 65568 | tf_op jit(solution)/shard_map/ppermute | solution.py:73
  15.1 6.1 %collective-permute-done.1 = bf16[128,256]{1,0:T(8,128)(2,1)S(1)} collective-permute-done((bf16[128,256]{1,0:T(8,128)(2,1)S(1)}, bf16[128,256]{1,0:T(8,128)(2,1)S(1)}, u32[]{:S(2)}, u32[]{:S(2)}) %collective-permute-start.1) | collective-permute-done | bytes 65568 | tf_op jit(solution)/shard_map/ppermute | solution.py:73
  21.8 5.4 %collective-permute-done.2 = bf16[128,256]{1,0:T(8,128)(2,1)S(1)} collective-permute-done((bf16[128,256]{1,0:T(8,128)(2,1)S(1)}, bf16[128,256]{1,0:T(8,128)(2,1)S(1)}, u32[]{:S(2)}, u32[]{:S(2)}) %collective-permute-start.2) | collective-permute-done | bytes 65568 | tf_op jit(solution)/shard_map/ppermute | solution.py:73
  27.2 2.3 %fusion.25 = bf16[512,256]{1,0:T(8,128)(2,1)S(1)} fusion(s32[]{:T(128)S(6)} %select_n.69, bf16[128,256]{1,0:T(8,128)(2,1)S(1)} %collective-permute-done.2, bf16[128,256]{1,0:T(8,128)(2,1)S(1)} %collective-permute-done.1, bf16[128,256]{1,0:T(8,128)(2,1)S(1)} %collective-permute-done, bf16[128,256]{1,0:T(8,128)(2,1)S(1)} %fusion.14), kind=kLoop, calls=%fused_computation.54 | loop fusion | flops 2097152 | bytes 524292 | tf_op jit(solution)/shard_map/jit(_roll_dynamic)/concatenate | solution.py:76
  29.6 17.7 %while.28 = (s32[]{:T(128)}, f32[4,128,256]{2,0,1:T(4,128)S(1)}, f32[4,32]{1,0:T(4,128)S(1)}, bf16[32,128,128]{2,1,0:T(8,128)(2,1)}, s32[32]{0:T(128)}, /*index=...) while((s32[]{:T(128)}, f32[4,128,256]{2,0,1:T(4,128)S(1)}, ...), condition=%wide.region_1.3_spmd.clone, body=%wide.region_0.2_spmd.clone.sunk | while | flops 79954976 | bytes 4985641 | solution.py:94
  30.9 1.2 fusion.67
  32.1 1.8 %convolution_add_fusion.7 = f32[4,128,256]{2,0,1:T(4,128)S(1)} fusion(f32[8,128,256]{2,1,0:T(8,128)S(1)} %fusion.67, f32[4,128,256]{2,0,1:T(4,128)S(1)} %get-tuple-element.381, pred[]{:T(512)S(6)} %compare.7, f32[4,32]{1,0:T(4,128)S(1)} %get-tuple-element.392, s32[]{:T(128)S(6)} %select_n.94), kind=kOutput, calls=%fused_computation.2.clone.1 | convolution fusion | flops 12845056 | bytes 2097669 | tf_op jit(solution)/shard_map/while/body/eval_jaxpr/sk,kaf->saf/dot_general | solution.py:89
  35.3 1.2 fusion.67
  36.6 1.8 %convolution_add_fusion.7 = f32[4,128,256]{2,0,1:T(4,128)S(1)} fusion(f32[8,128,256]{2,1,0:T(8,128)S(1)} %fusion.67, f32[4,128,256]{2,0,1:T(4,128)S(1)} %get-tuple-element.381, pred[]{:T(512)S(6)} %compare.7, f32[4,32]{1,0:T(4,128)S(1)} %get-tuple-element.392, s32[]{:T(128)S(6)} %select_n.94), kind=kOutput, calls=%fused_computation.2.clone.1 | convolution fusion | flops 12845056 | bytes 2097669 | tf_op jit(solution)/shard_map/while/body/eval_jaxpr/sk,kaf->saf/dot_general | solution.py:89
  39.8 1.2 fusion.67
  41.0 1.8 %convolution_add_fusion.7 = f32[4,128,256]{2,0,1:T(4,128)S(1)} fusion(f32[8,128,256]{2,1,0:T(8,128)S(1)} %fusion.67, f32[4,128,256]{2,0,1:T(4,128)S(1)} %get-tuple-element.381, pred[]{:T(512)S(6)} %compare.7, f32[4,32]{1,0:T(4,128)S(1)} %get-tuple-element.392, s32[]{:T(128)S(6)} %select_n.94), kind=kOutput, calls=%fused_computation.2.clone.1 | convolution fusion | flops 12845056 | bytes 2097669 | tf_op jit(solution)/shard_map/while/body/eval_jaxpr/sk,kaf->saf/dot_general | solution.py:89
  44.2 1.2 fusion.67
  45.5 1.8 %convolution_add_fusion.7 = f32[4,128,256]{2,0,1:T(4,128)S(1)} fusion(f32[8,128,256]{2,1,0:T(8,128)S(1)} %fusion.67, f32[4,128,256]{2,0,1:T(4,128)S(1)} %get-tuple-element.381, pred[]{:T(512)S(6)} %compare.7, f32[4,32]{1,0:T(4,128)S(1)} %get-tuple-element.392, s32[]{:T(128)S(6)} %select_n.94), kind=kOutput, calls=%fused_computation.2.clone.1 | convolution fusion | flops 12845056 | bytes 2097669 | tf_op jit(solution)/shard_map/while/body/eval_jaxpr/sk,kaf->saf/dot_general | solution.py:89
  47.3 0.9 copy.15
  49.9 10.2 %all-reduce = f32[512]{0:T(512)S(1)} all-reduce(f32[512]{0:T(512)S(1)} %convolution_bitcast_fusion), channel_id=3, replica_groups=mesh['layer'=2,'row'=4,'rep'=4] {'rep'}, use_global_device_ids=true, to_apply=%region_4.6.clone | all-reduce | flops 512 | bytes 4096
  60.4 11.6 %reduce-scatter.3.cloned.1.call-done = f32[128,256]{1,0:T(8,128)} async-done(((f32[512,256]{1,0:T(8,128)}), f32[128,256]{1,0:T(8,128)}) %reduce-scatter.3.cloned.1.call-update) | async-done | bytes 131088 | tf_op jit(solution)/shard_map/reduce_scatter | solution.py:98
  72.0 1.2 maximum_reduce_fusion.1
  73.5 1.4 collective-permute-start.3
  75.8 1.5 %collective-permute-start.4 = (bf16[128,256]{1,0:T(8,128)(2,1)S(1)}, bf16[128,256]{1,0:T(8,128)(2,1)S(1)}, u32[]{:S(2)}, u32[]{:S(2)}) collective-permute-start(bf16[128,256]{1,0:T(8,128)(2,1)S(1)} %collective-permute-done.3), channel_id=1, source_target_pairs={{0,4},{4,8},{8,12},{12,0},{1,5},{5,9},{9,13},{13,1},{2,6},{6,10},{... | collective-permute-start | bytes 196616 | tf_op jit(solution)/shard_map/ppermute | solution.py:73
  77.3 4.6 %collective-permute-done.4 = bf16[128,256]{1,0:T(8,128)(2,1)S(1)} collective-permute-done((bf16[128,256]{1,0:T(8,128)(2,1)S(1)}, bf16[128,256]{1,0:T(8,128)(2,1)S(1)}, u32[]{:S(2)}, u32[]{:S(2)}) %collective-permute-start.4) | collective-permute-done | bytes 65568 | tf_op jit(solution)/shard_map/ppermute | solution.py:73
  81.9 6.1 %collective-permute-done.5 = bf16[128,256]{1,0:T(8,128)(2,1)S(1)} collective-permute-done((bf16[128,256]{1,0:T(8,128)(2,1)S(1)}, bf16[128,256]{1,0:T(8,128)(2,1)S(1)}, u32[]{:S(2)}, u32[]{:S(2)}) %collective-permute-start.5) | collective-permute-done | bytes 65568 | tf_op jit(solution)/shard_map/ppermute | solution.py:73
  88.0 6.1 %collective-permute-done.6 = bf16[128,256]{1,0:T(8,128)(2,1)S(1)} collective-permute-done((bf16[128,256]{1,0:T(8,128)(2,1)S(1)}, bf16[128,256]{1,0:T(8,128)(2,1)S(1)}, u32[]{:S(2)}, u32[]{:S(2)}) %collective-permute-start.6) | collective-permute-done | bytes 65568 | tf_op jit(solution)/shard_map/ppermute | solution.py:73
  94.1 2.3 %fusion.18 = bf16[512,256]{1,0:T(8,128)(2,1)S(1)} fusion(s32[]{:T(128)S(6)} %select_n.69, bf16[128,256]{1,0:T(8,128)(2,1)S(1)} %collective-permute-done.6, bf16[128,256]{1,0:T(8,128)(2,1)S(1)} %collective-permute-done.5, bf16[128,256]{1,0:T(8,128)(2,1)S(1)} %collective-permute-done.4, bf16[128,256]{1,0:T(8,128)(2,1)S(1)} %collective-permute-done.3), kind=kLoop, calls=%fused_computation.47 | loop fusion | flops 2097152 | bytes 524292 | tf_op jit(solution)/shard_map/jit(_roll_dynamic)/concatenate | solution.py:76
  96.4 13.9 %while.29 = (s32[]{:T(128)}, f32[4,128,256]{2,0,1:T(4,128)S(1)}, f32[4,32]{1,0:T(4,128)S(1)}, bf16[32,128,128]{2,1,0:T(8,128)(2,1)S(1)}, s32[32]{0:T(128)}, /*in...) while((s32[]{:T(128)}, f32[4,128,256]{2,0,1:T(4,128)S(1)}, ...), condition=%wide.region_8.10_spmd.clone, body=%wide.region_7.9_spmd.clone.sunk | while | flops 79954976 | bytes 4985641 | solution.py:94
  98.1 1.8 %convolution_add_fusion.8 = f32[4,128,256]{2,0,1:T(4,128)S(1)} fusion(f32[8,128,256]{2,1,0:T(8,128)S(1)} %fusion.72, f32[4,128,256]{2,0,1:T(4,128)S(1)} %get-tuple-element.411, pred[]{:T(512)S(6)} %compare.8, f32[4,32]{1,0:T(4,128)S(1)} %get-tuple-element.422, s32[]{:T(128)S(6)} %select_n.96), kind=kOutput, calls=%fused_computation.12.clone.1 | convolution fusion | flops 12845056 | bytes 2097669 | tf_op jit(solution)/shard_map/while/body/eval_jaxpr/sk,kaf->saf/dot_general | solution.py:89
  101.5 1.8 %convolution_add_fusion.8 = f32[4,128,256]{2,0,1:T(4,128)S(1)} fusion(f32[8,128,256]{2,1,0:T(8,128)S(1)} %fusion.72, f32[4,128,256]{2,0,1:T(4,128)S(1)} %get-tuple-element.411, pred[]{:T(512)S(6)} %compare.8, f32[4,32]{1,0:T(4,128)S(1)} %get-tuple-element.422, s32[]{:T(128)S(6)} %select_n.96), kind=kOutput, calls=%fused_computation.12.clone.1 | convolution fusion | flops 12845056 | bytes 2097669 | tf_op jit(solution)/shard_map/while/body/eval_jaxpr/sk,kaf->saf/dot_general | solution.py:89
  105.0 1.8 %convolution_add_fusion.8 = f32[4,128,256]{2,0,1:T(4,128)S(1)} fusion(f32[8,128,256]{2,1,0:T(8,128)S(1)} %fusion.72, f32[4,128,256]{2,0,1:T(4,128)S(1)} %get-tuple-element.411, pred[]{:T(512)S(6)} %compare.8, f32[4,32]{1,0:T(4,128)S(1)} %get-tuple-element.422, s32[]{:T(128)S(6)} %select_n.96), kind=kOutput, calls=%fused_computation.12.clone.1 | convolution fusion | flops 12845056 | bytes 2097669 | tf_op jit(solution)/shard_map/while/body/eval_jaxpr/sk,kaf->saf/dot_general | solution.py:89
  108.5 1.8 %convolution_add_fusion.8 = f32[4,128,256]{2,0,1:T(4,128)S(1)} fusion(f32[8,128,256]{2,1,0:T(8,128)S(1)} %fusion.72, f32[4,128,256]{2,0,1:T(4,128)S(1)} %get-tuple-element.411, pred[]{:T(512)S(6)} %compare.8, f32[4,32]{1,0:T(4,128)S(1)} %get-tuple-element.422, s32[]{:T(128)S(6)} %select_n.96), kind=kOutput, calls=%fused_computation.12.clone.1 | convolution fusion | flops 12845056 | bytes 2097669 | tf_op jit(solution)/shard_map/while/body/eval_jaxpr/sk,kaf->saf/dot_general | solution.py:89
  111.3 22.5 %reduce-scatter.5.cloned.1.call-done = f32[128,256]{1,0:T(8,128)} async-done(((f32[512,256]{1,0:T(8,128)}), f32[128,256]{1,0:T(8,128)}) %reduce-scatter.5.cloned.1.call-update) | async-done | bytes 131088 | tf_op jit(solution)/shard_map/reduce_scatter | solution.py:102
  133.8 1.1 fusion.29
  (86 shorter events, 17.1 us)
Async XLA Ops:
  6.5 65.5 %copy-start = (bf16[1,256,256]{2,1,0:T(8,128)(2,1)S(1)}, bf16[1,256,256]{2,1,0:T(8,128)(2,1)}, u32[]{:S(2)}) copy-start(bf16[1,256,256]{2,1,0:T(8,128)(2,1)} %param.20) | copy-start | bytes 393220
  6.5 65.5 %reduce-scatter.3.cloned.1.call-start = ((), (), s32[]{:S(2)}) async-start(), calls=%async_computation.2 | async-start | bytes 655360 | tf_op jit(solution)/shard_map/reduce_scatter | solution.py:98
  7.7 21.8 %copy-start.4 = (bf16[128,256]{1,0:T(8,128)(2,1)}, bf16[128,256]{1,0:T(8,128)(2,1)S(1)}, u32[]{:S(2)}) copy-start(bf16[128,256]{1,0:T(8,128)(2,1)S(1)} %fusion.14) | copy-start | bytes 196612
  7.7 7.4 %collective-permute-start = (bf16[128,256]{1,0:T(8,128)(2,1)S(1)}, bf16[128,256]{1,0:T(8,128)(2,1)S(1)}, u32[]{:S(2)}, u32[]{:S(2)}) collective-permute-start(bf16[128,256]{1,0:T(8,128)(2,1)S(1)} %fusion.14), channel_id=1, source_target_pairs={{0,4},{4,8},{8,12},{12,0},{1,5},{5,9},{9,13},{13,1},{2,6},{6,10},{... | collective-permute-start | bytes 196616 | tf_op jit(solution)/shard_map/ppermute | solution.py:73
  15.1 6.1 %collective-permute-start.1 = (bf16[128,256]{1,0:T(8,128)(2,1)S(1)}, bf16[128,256]{1,0:T(8,128)(2,1)S(1)}, u32[]{:S(2)}, u32[]{:S(2)}) collective-permute-start(bf16[128,256]{1,0:T(8,128)(2,1)S(1)} %collective-permute-done), channel_id=1, source_target_pairs={{0,4},{4,8},{8,12},{12,0},{1,5},{5,9},{9,13},{13,1},{2,6},{6,10},{... | collective-permute-start | bytes 196616 | tf_op jit(solution)/shard_map/ppermute | solution.py:73
  21.2 6.1 %collective-permute-start.2 = (bf16[128,256]{1,0:T(8,128)(2,1)S(1)}, bf16[128,256]{1,0:T(8,128)(2,1)S(1)}, u32[]{:S(2)}, u32[]{:S(2)}) collective-permute-start(bf16[128,256]{1,0:T(8,128)(2,1)S(1)} %collective-permute-done.1), channel_id=1, source_target_pairs={{0,4},{4,8},{8,12},{12,0},{1,5},{5,9},{9,13},{13,1},{2,6},{6,10},{... | collective-permute-start | bytes 196616 | tf_op jit(solution)/shard_map/ppermute | solution.py:73
  47.3 1.0 copy-start.14
  47.3 2.1 %copy-start.1 = (bf16[32,128,128]{2,1,0:T(8,128)(2,1)S(1)}, bf16[32,128,128]{2,1,0:T(8,128)(2,1)}, u32[]{:S(2)}) copy-start(bf16[32,128,128]{2,1,0:T(8,128)(2,1)} %get-tuple-element.432) | copy-start | bytes 3145732
  48.2 1.6 %copy-start.11 = (s32[1,1,32]{2,1,0:T(1,128)S(1)}, s32[1,1,32]{2,1,0:T(1,128)}, u32[]{:S(2)}) copy-start(s32[1,1,32]{2,1,0:T(1,128)} %param.23) | copy-start | bytes 388
  48.2 12.0 %copy-start.5 = (bf16[128,256]{1,0:T(8,128)(2,1)S(1)}, bf16[128,256]{1,0:T(8,128)(2,1)}, u32[]{:S(2)}) copy-start(bf16[128,256]{1,0:T(8,128)(2,1)} %copy-done.4) | copy-start | bytes 196612
  48.2 12.0 %copy-start.6 = (bf16[1,256,256]{2,1,0:T(8,128)(2,1)S(1)}, bf16[1,256,256]{2,1,0:T(8,128)(2,1)}, u32[]{:S(2)}) copy-start(bf16[1,256,256]{2,1,0:T(8,128)(2,1)} %param.19) | copy-start | bytes 393220
  48.3 85.6 %reduce-scatter.5.cloned.1.call-start = ((), (), s32[]{:S(2)}) async-start(), calls=%async_computation.3 | async-start | bytes 655360 | tf_op jit(solution)/shard_map/reduce_scatter | solution.py:102
  48.3 25.1 %copy-start.10 = (f32[256]{0:T(256)S(1)}, f32[256]{0:T(256)}, u32[]{:S(2)}) copy-start(f32[256]{0:T(256)} %param.21) | copy-start | bytes 3076
  60.2 21.7 %copy-start.12 = (f32[128]{0:T(128)}, f32[128]{0:T(128)S(1)}, u32[]{:S(2)}) copy-start(f32[128]{0:T(128)S(1)} %dynamic-slice_rsqrt_fusion) | copy-start | bytes 1540
  73.2 23.2 %copy-start.2 = (f32[128,256]{1,0:T(8,128)}, f32[128,256]{1,0:T(8,128)S(1)}, u32[]{:S(2)}) copy-start(f32[128,256]{1,0:T(8,128)S(1)} %get-tuple-element.293) | copy-start | bytes 393220
  73.5 2.3 %collective-permute-start.3 = (bf16[128,256]{1,0:T(8,128)(2,1)S(1)}, bf16[128,256]{1,0:T(8,128)(2,1)S(1)}, u32[]{:S(2)}, u32[]{:S(2)}) collective-permute-start(bf16[128,256]{1,0:T(8,128)(2,1)S(1)} %fusion.35), channel_id=1, source_target_pairs={{0,16},{1,17},{2,18},{3,19},{4,20},{5,21},{6,22},{7,23},{8,24},{9,... | collective-permute-start | bytes 196616 | tf_op jit(solution)/shard_map/ppermute | solution.py:10
  75.8 20.6 %copy-start.8 = (bf16[128,256]{1,0:T(8,128)(2,1)}, bf16[128,256]{1,0:T(8,128)(2,1)S(1)}, u32[]{:S(2)}) copy-start(bf16[128,256]{1,0:T(8,128)(2,1)S(1)} %collective-permute-done.3) | copy-start | bytes 196612
  75.8 6.1 %collective-permute-start.4 = (bf16[128,256]{1,0:T(8,128)(2,1)S(1)}, bf16[128,256]{1,0:T(8,128)(2,1)S(1)}, u32[]{:S(2)}, u32[]{:S(2)}) collective-permute-start(bf16[128,256]{1,0:T(8,128)(2,1)S(1)} %collective-permute-done.3), channel_id=1, source_target_pairs={{0,4},{4,8},{8,12},{12,0},{1,5},{5,9},{9,13},{13,1},{2,6},{6,10},{... | collective-permute-start | bytes 196616 | tf_op jit(solution)/shard_map/ppermute | solution.py:73
  81.9 6.1 %collective-permute-start.5 = (bf16[128,256]{1,0:T(8,128)(2,1)S(1)}, bf16[128,256]{1,0:T(8,128)(2,1)S(1)}, u32[]{:S(2)}, u32[]{:S(2)}) collective-permute-start(bf16[128,256]{1,0:T(8,128)(2,1)S(1)} %collective-permute-done.4), channel_id=1, source_target_pairs={{0,4},{4,8},{8,12},{12,0},{1,5},{5,9},{9,13},{13,1},{2,6},{6,10},{... | collective-permute-start | bytes 196616 | tf_op jit(solution)/shard_map/ppermute | solution.py:73
  88.0 6.1 %collective-permute-start.6 = (bf16[128,256]{1,0:T(8,128)(2,1)S(1)}, bf16[128,256]{1,0:T(8,128)(2,1)S(1)}, u32[]{:S(2)}, u32[]{:S(2)}) collective-permute-start(bf16[128,256]{1,0:T(8,128)(2,1)S(1)} %collective-permute-done.5), channel_id=1, source_target_pairs={{0,4},{4,8},{8,12},{12,0},{1,5},{5,9},{9,13},{13,1},{2,6},{6,10},{... | collective-permute-start | bytes 196616 | tf_op jit(solution)/shard_map/ppermute | solution.py:73
  110.3 23.5 %copy-start.13 = (f32[128]{0:T(128)S(1)}, f32[128]{0:T(128)}, u32[]{:S(2)}) copy-start(f32[128]{0:T(128)} %copy-done.12) | copy-start | bytes 1540
  110.3 24.6 %copy-start.7 = (bf16[1,256,256]{2,1,0:T(8,128)(2,1)S(1)}, bf16[1,256,256]{2,1,0:T(8,128)(2,1)}, u32[]{:S(2)}) copy-start(bf16[1,256,256]{2,1,0:T(8,128)(2,1)} %param.19) | copy-start | bytes 393220
  110.3 24.6 %copy-start.9 = (bf16[128,256]{1,0:T(8,128)(2,1)S(1)}, bf16[128,256]{1,0:T(8,128)(2,1)}, u32[]{:S(2)}) copy-start(bf16[128,256]{1,0:T(8,128)(2,1)} %copy-done.8) | copy-start | bytes 196612
  110.4 25.0 %copy-start.3 = (f32[128,256]{1,0:T(8,128)S(1)}, f32[128,256]{1,0:T(8,128)}, u32[]{:S(2)}) copy-start(f32[128,256]{1,0:T(8,128)} %copy-done.2) | copy-start | bytes 393220
Sparse Core Ops, SparseCore 0:
  48.4 23.5 reduce-scatter.2
  111.4 22.3 reduce-scatter.4
